TPU v7x, 256 devices: a whole 4x4x8 slice. The times are simulated.
256 devices in a mesh: tile: 64 (over z, y_lo, x), mode: 4 (over y_hi, core).
Axes of the slice: x: 4, y: 4 (y_hi: 2, y_lo: 2; y = y_hi * 2 + y_lo), z: 8, core: 2. Of those that a mesh axis runs over, the one named last changes fastest.
Arguments:
- object_tiles: float32 [64, 2, 2, 256, 256], P('tile'), may hold values from -6 to 6
- object_previous: float32 [64, 2, 2, 256, 256], P('tile'), may hold values from -6 to 6
- probe: float32 [4, 8, 2, 256, 256], P(None, 'mode', None, 'tile'), may hold values from -2 to 2
- probe_previous: float32 [4, 8, 2, 256, 256], P(None, 'mode', None, 'tile'), may hold values from -6 to 6
- patterns: float32 [128, 256, 256], P('tile'), may hold values from 0 to 2
- offsets: int32 [2, 128], P(None, 'tile'), may hold values from 0 to 255
- scan_of_slot: int32 [128], P('tile'), may hold values from 0 to 3
- tile_load: int32 [64], P('tile'), may hold values from 1 to 2, as said below
- step_sizes: int32 [2], replicated, may hold values from 128 to 511
- object_norm_before: float32 [1], replicated, may hold values from 0.1 to 0.4
- probe_norm_before: float32 [1], replicated, may hold values from 12 to 64
Outputs:
- new_object: float32 [64, 2, 2, 256, 256], P('tile')
- object_direction: float32 [64, 2, 2, 256, 256], P('tile')
- new_probe: float32 [4, 8, 2, 256, 256], P(None, 'mode', None, 'tile')
- probe_direction: float32 [4, 8, 2, 256, 256], P(None, 'mode', None, 'tile')
Inputs may be any that keep to these rules, and one draw needn't show every extreme that they name: `tile_load`: every tile holds 1 to 2 used slots, and some tile holds exactly 2.
All inputs are finite; a program needn't handle non-finite values.
Results may differ from a plain program's by a relative error of at most 0.024.
Values may be sent and summed in bfloat16 or wider, within the bound.
No kernel may reach another device: no remote copies, remote signals or barrier semaphores. Data moves between devices by JAX's collectives and lax.ppermute only.
A program may use at most 64 MiB of HBM per device.

v0:
```python
import math
import jax
import jax.numpy as jnp
from jax import lax
from jax.sharding import PartitionSpec as P

TGX = 8
MODES = 8
SCAN_COUNT = 4
residual_weight = 2.0


def from_behind(block, axis, distance):
    devices = range(lax.axis_size(axis))
    route = [(i - distance, i) for i in devices if i - distance in devices]
    return lax.ppermute(block, axis, route)


def table_pair(width):
    index_row = jnp.arange(width, dtype=jnp.int32)
    product = index_row[:, None] * index_row[None, :] % width
    angle = product.astype(jnp.float32) * (2.0 * math.pi / width)
    factor = 1.0 / math.sqrt(width)
    cosine = (jnp.cos(angle) * factor).astype(jnp.bfloat16)
    sine = (-jnp.sin(angle) * factor).astype(jnp.bfloat16)
    index_free = jnp.where(index_row < width // 2, index_row, index_row - width).astype(jnp.float32)
    phase = (
        index_free[:, None] * index_free[:, None] + index_free[None, :] * index_free[None, :]
    ) * (math.pi / (4.0 * width))
    return (cosine, sine, jnp.cos(phase), jnp.sin(phase))


def right_product(left_data, table):
    return jnp.einsum("...jk,kl->...jl", left_data, table, preferred_element_type=jnp.float32)


def left_product(table, right_data):
    return jnp.einsum("ij,...jl->...il", table, right_data, preferred_element_type=jnp.float32)


def transform(wave_re, wave_im, tables, inverse):
    cosine = tables[0]
    sine = -tables[1] if inverse else tables[1]
    first_re = (right_product(wave_re, cosine) - right_product(wave_im, sine)).astype(jnp.bfloat16)
    first_im = (right_product(wave_re, sine) + right_product(wave_im, cosine)).astype(jnp.bfloat16)
    out_re = (left_product(cosine, first_re) - left_product(sine, first_im)).astype(jnp.bfloat16)
    out_im = (left_product(sine, first_re) + left_product(cosine, first_im)).astype(jnp.bfloat16)
    return (out_re, out_im)


def complex_times(first_re, first_im, second_re, second_im):
    first_portion = first_re.astype(jnp.float32)
    b_part = first_im.astype(jnp.float32)
    c_part = second_re.astype(jnp.float32)
    d_part = second_im.astype(jnp.float32)
    return (first_portion * c_part - b_part * d_part, first_portion * d_part + b_part * c_part)


def conj_times(first_re, first_im, second_re, second_im):
    first_portion = first_re.astype(jnp.float32)
    b_part = first_im.astype(jnp.float32)
    c_part = second_re.astype(jnp.float32)
    d_part = second_im.astype(jnp.float32)
    return (first_portion * c_part + b_part * d_part, first_portion * d_part - b_part * c_part)


def propagate(wave_re, wave_im, tables, adjoint):
    spec_re, spec_im = transform(wave_re, wave_im, tables, False)
    kernel_im = -tables[3] if adjoint else tables[3]
    moved_re, moved_im = complex_times(spec_re, spec_im, tables[2], kernel_im)
    return transform(moved_re.astype(jnp.bfloat16), moved_im.astype(jnp.bfloat16), tables, True)


def body(
    object_tiles,
    object_previous,
    probe,
    probe_previous,
    patterns,
    offsets,
    scan_of_slot,
    tile_load,
    step_sizes,
    object_norm_before,
    probe_norm_before,
):
    tile_count = lax.axis_size("tile")
    mode_count = lax.axis_size("mode")
    slots = patterns.shape[0]
    width = patterns.shape[1]
    layers = object_tiles.shape[1]
    tile_side = object_tiles.shape[3]
    scans = probe.shape[0]
    tables = table_pair(width)
    own_tile = object_tiles[0].astype(jnp.bfloat16)
    east_part = from_behind(own_tile, "tile", -1)
    upper = jnp.concatenate([own_tile, east_part], axis=3)
    lower = from_behind(upper, "tile", -TGX)
    region = jnp.concatenate([upper, lower], axis=2)
    gathered = lax.all_gather(probe.astype(jnp.bfloat16), "tile", axis=3, tiled=True)
    valid_mask = (jnp.arange(slots, dtype=jnp.int32) < tile_load[0]).astype(jnp.float32)

    def cut_patch(row_start, col_start):
        return lax.dynamic_slice(region, (0, 0, row_start, col_start), (layers, 2, width, width))

    patches = jax.vmap(cut_patch)(offsets[0], offsets[1])
    probe_pick = jnp.take(gathered, scan_of_slot, axis=0)
    wave_re = probe_pick[:, :, 0]
    wave_im = probe_pick[:, :, 1]
    incident = []
    for layer_index in range(layers):
        incident.append((wave_re, wave_im))
        next_re, next_im = complex_times(
            wave_re, wave_im, patches[:, None, layer_index, 0], patches[:, None, layer_index, 1]
        )
        wave_re = next_re.astype(jnp.bfloat16)
        wave_im = next_im.astype(jnp.bfloat16)
        if layer_index + 1 < layers:
            wave_re, wave_im = propagate(wave_re, wave_im, tables, False)
    far_re, far_im = transform(wave_re, wave_im, tables, False)
    far_re32 = far_re.astype(jnp.float32)
    far_im32 = far_im.astype(jnp.float32)
    partial_power = jnp.sum(far_re32 * far_re32 + far_im32 * far_im32, axis=1)
    power = lax.psum(partial_power, "mode")
    misfit = (power - patterns) * valid_mask[:, None, None]
    back_re = (residual_weight * misfit[:, None] * far_re32).astype(jnp.bfloat16)
    back_im = (residual_weight * misfit[:, None] * far_im32).astype(jnp.bfloat16)
    back_re, back_im = transform(back_re, back_im, tables, True)
    slice_terms = [None] * layers
    probe_terms = None
    for layer_index in reversed(range(layers)):
        inc_re, inc_im = incident[layer_index]
        grad_re, grad_im = conj_times(inc_re, inc_im, back_re, back_im)
        slice_terms[layer_index] = jnp.stack(
            [jnp.sum(grad_re, axis=1), jnp.sum(grad_im, axis=1)], axis=1
        )
        carry_re, carry_im = conj_times(
            patches[:, None, layer_index, 0], patches[:, None, layer_index, 1], back_re, back_im
        )
        if layer_index > 0:
            back_re, back_im = propagate(
                carry_re.astype(jnp.bfloat16), carry_im.astype(jnp.bfloat16), tables, True
            )
        else:
            probe_terms = jnp.stack([carry_re, carry_im], axis=2)
    slot_grads = jnp.stack(slice_terms, axis=1)
    region_grad = jnp.zeros((layers, 2, 2 * tile_side, 2 * tile_side), jnp.float32)
    for slot_index in range(slots):
        starts = (0, 0, offsets[0, slot_index], offsets[1, slot_index])
        current = lax.dynamic_slice(region_grad, starts, (layers, 2, width, width))
        region_grad = lax.dynamic_update_slice(
            region_grad, current + slot_grads[slot_index], starts
        )
    region_grad = lax.psum(region_grad.astype(jnp.bfloat16), "mode").astype(jnp.float32)
    from_above = from_behind(
        region_grad[:, :, tile_side:, :].astype(jnp.bfloat16), "tile", TGX
    ).astype(jnp.float32)
    upper_grad = region_grad[:, :, :tile_side, :] + from_above
    from_left = from_behind(upper_grad[:, :, :, tile_side:].astype(jnp.bfloat16), "tile", 1).astype(
        jnp.float32
    )
    tile_grad = upper_grad[:, :, :, :tile_side] + from_left
    scan_onehot = (scan_of_slot[:, None] == jnp.arange(scans, dtype=jnp.int32)[None, :]).astype(
        jnp.float32
    )
    probe_local = jnp.einsum(
        "cs,cmrij->smrij", scan_onehot, probe_terms, precision=lax.Precision.HIGHEST
    )
    probe_grad = lax.psum_scatter(probe_local, "tile", scatter_dimension=3, tiled=True)
    object_sum = jnp.sum(tile_grad * tile_grad) / float(mode_count)
    probe_sum = jnp.sum(probe_grad * probe_grad)
    object_total, probe_total = lax.psum((object_sum, probe_sum), ("tile", "mode"))
    object_square = object_total / float(tile_count * layers * 2 * tile_side * tile_side)
    probe_square = probe_total / float(SCAN_COUNT * MODES * 2 * width * width)
    object_direction = -tile_grad[None] + object_square / object_norm_before[0] * object_previous
    new_object = object_tiles + step_sizes[0].astype(jnp.float32) / 1024.0 * object_direction
    probe_direction = -probe_grad + probe_square / probe_norm_before[0] * probe_previous
    new_probe = probe + step_sizes[1].astype(jnp.float32) / 16384.0 * probe_direction
    return (new_object, object_direction, new_probe, probe_direction)


def solution(mesh):
    return jax.shard_map(
        body,
        mesh=mesh,
        in_specs=(
            P("tile", None, None, None, None),
            P("tile", None, None, None, None),
            P(None, "mode", None, "tile", None),
            P(None, "mode", None, "tile", None),
            P("tile", None, None),
            P(None, "tile"),
            P("tile"),
            P("tile"),
            P(),
            P(),
            P(),
        ),
        out_specs=(
            P("tile", None, None, None, None),
            P("tile", None, None, None, None),
            P(None, "mode", None, "tile", None),
            P(None, "mode", None, "tile", None),
        ),
        check_vma=False,
    )
```

profile of v0, /device:TPU:1, one launch (start us, length us, event | category | flops | bytes accessed | tf_op | source)
XLA Modules:
  0.0 1247.7 jit_solution(10554642321168706119)
XLA Ops:
  12.1 11.3 collective-permute-done
  26.9 28.3 %collective-permute-done.1 = bf16[2,2,256,512]{3,2,1,0:T(8,128)(2,1)} collective-permute-done((bf16[2,2,256,512]{3,2,1,0:T(8,128)(2,1)S(1)}, bf16[2,2,256,512]{3,2,1,0:T(8,128)(2,1)}, u32[]{:S(2)}, u32[]{:S(2)}) %collective-permute-start.1) | collective-permute-done | bytes 1048608 | tf_op jit(solution)/shard_map/ppermute | solution.py:16
  56.6 6.0 while.1
  66.4 200.3 %all-gather.2.cloned.1.call-done = bf16[4,2,2,256,256]{4,0,2,1,3:T(4,128)(2,1)} async-done(((bf16[4,2,2,4,256]{4,0,2,1,3:T(4,128)(2,1)}), bf16[4,2,2,256,256]{4,0,2,1,3:T(4,128)(2,1)}) %all-gather.2.cloned.1.call-update) | async-done | bytes 2097168 | tf_op jit(solution)/shard_map/all_gather | solution.py:100
  292.4 2.4 add_convert_fusion.2
  317.1 82.1 %all-reduce.6.cloned.1.call-done = f32[2,256,256]{1,2,0:T(8,128)} async-done(((f32[2,256,256]{1,2,0:T(8,128)}), f32[2,256,256]{1,2,0:T(8,128)}) %all-reduce.6.cloned.1.call-update) | async-done | bytes 524304 | tf_op jit(solution)/shard_map/psum | solution.py:124
  409.8 2.5 add_reduce_fusion
  431.7 3.0 add_bitcast_fusion
  435.0 2.5 broadcast_in_dim.11
  437.4 11.2 dynamic_update_slice.6
  450.4 12.3 dynamic_update_slice.7
  462.7 3.9 convert_element_type.598
  469.6 3.1 copy.197
  472.7 6.6 fusion.156
  479.4 50.8 %all-reduce.8.cloned.1.call-done = bf16[2,2,512,512]{2,3,1,0:T(8,128)(2,1)} async-done(((bf16[2,2,512,512]{2,3,1,0:T(8,128)(2,1)}), bf16[2,2,512,512]{2,3,1,0:T(8,128)(2,1)}) %all-reduce.8.cloned.1.call-update) | async-done | bytes 2097168 | tf_op jit(solution)/shard_map/psum | solution.py:154
  531.7 3.4 collective-permute-start.2
  535.1 22.3 %collective-permute-done.2 = bf16[2,2,256,512]{2,3,1,0:T(8,128)(2,1)S(1)} collective-permute-done((bf16[2,2,256,512]{2,3,1,0:T(8,128)(2,1)S(1)}, bf16[2,2,256,512]{2,3,1,0:T(8,128)(2,1)S(1)}, u32[]{:S(2)}, u32[]{:S(2)}) %collective-permute-start.2) | collective-permute-done | bytes 1048608 | tf_op jit(solution)/shard_map/ppermute | solution.py:16
  558.4 3.9 collective-permute-start.3
  566.9 2.6 copy.195
  570.8 2.8 collective-permute-done.3
  576.2 531.9 %all-reduce.10.cloned.1.call-done = f32[4,2,2,256,256]{4,0,3,2,1:T(4,128)} async-done(((f32[4,2,2,256,256]{4,0,3,2,1:T(4,128)}), f32[4,2,2,256,256]{4,0,3,2,1:T(4,128)}) %all-reduce.10.cloned.1.call-update) | async-done | bytes 4194320
  1109.6 120.8 %all-reduce.1 = (f32[]{:T(128)}, f32[]{:T(128)}) all-reduce(f32[]{:T(128)S(6)} %div.27, f32[]{:T(128)} %multiply_reduce_fusion.1), channel_id=1, replica_groups=mesh['tile'=64,'mode'=4] {'tile','mode'}, use_global_device_ids=true, to_apply=%region_8.9 | all-reduce | flops 2 | bytes 16 | tf_op jit(solution)/shard_map/psum | solution.py:172
  1234.0 2.9 multiply_add_fusion
  1237.0 2.6 copy.200
  (157 shorter events, 105.9 us)
Async XLA Ops:
  7.2 17.8 %copy-start.23 = (s32[2]{0:T(128)S(1)}, s32[2]{0:T(128)}, u32[]{:S(2)}) copy-start(s32[2]{0:T(128)} %param.17) | copy-start | bytes 28
  7.2 259.5 %all-gather.2.cloned.1.call-start = ((), (), s32[]{:S(2)}) async-start(), calls=%async_computation | async-start | bytes 2129920 | tf_op jit(solution)/shard_map/all_gather | solution.py:100
  8.7 390.5 %all-reduce.6.cloned.1.call-start = ((), (), s32[]{:S(2)}) async-start(), calls=%async_computation.1 | async-start | bytes 1048576 | tf_op jit(solution)/shard_map/psum | solution.py:124
  10.1 13.3 %collective-permute-start = (bf16[2,2,256,256]{3,2,1,0:T(8,128)(2,1)S(1)}, bf16[2,2,256,256]{3,2,1,0:T(8,128)(2,1)S(1)}, u32[]{:S(2)}, u32[]{:S(2)}) collective-permute-start(bf16[2,2,256,256]{3,2,1,0:T(8,128)(2,1)S(1)} %convert_bitcast_fusion), channel_id=1, source_target_pairs={{4,0},{8,4},{12,8},{16,12},{20,16},{24,20},{28,24},{32,28},{36,32}... | collective-permute-start | bytes 1572872 | tf_op jit(solution)/shard_map/ppermute | solution.py:16
  23.5 31.7 %collective-permute-start.1 = (bf16[2,2,256,512]{3,2,1,0:T(8,128)(2,1)S(1)}, bf16[2,2,256,512]{3,2,1,0:T(8,128)(2,1)}, u32[]{:S(2)}, u32[]{:S(2)}) collective-permute-start(bf16[2,2,256,512]{3,2,1,0:T(8,128)(2,1)S(1)} %pad_maximum_fusion.3), channel_id=1, source_target_pairs={{32,0},{36,4},{40,8},{44,12},{48,16},{52,20},{56,24},{60,28},{64,3... | collective-permute-start | bytes 3145736 | tf_op jit(solution)/shard_map/ppermute | solution.py:16
  64.2 208.5 %copy-start.2 = (f32[2,256,256]{1,2,0:T(8,128)}, f32[2,256,256]{1,2,0:T(8,128)S(1)}, u32[]{:S(2)}) copy-start(f32[2,256,256]{1,2,0:T(8,128)S(1)} %copy.142) | copy-start | bytes 1572868
  64.4 208.3 %copy-start.4 = (f32[2,256,256]{1,2,0:T(8,128)}, f32[2,256,256]{1,2,0:T(8,128)S(1)}, u32[]{:S(2)}) copy-start(f32[2,256,256]{1,2,0:T(8,128)S(1)} %copy.143) | copy-start | bytes 1572868
  289.9 2.5 copy-start.6
  289.9 2.5 copy-start.8
  306.3 224.0 %all-reduce.8.cloned.1.call-start = ((), (), s32[]{:S(2)}) async-start(), calls=%async_computation.2 | async-start | bytes 4194304 | tf_op jit(solution)/shard_map/psum | solution.py:154
  429.1 2.6 copy-start.1
  429.1 2.6 copy-start.3
  429.1 2.6 copy-start.5
  466.6 641.5 %all-reduce.10.cloned.1.call-start = ((), (), s32[]{:S(2)}) async-start(), calls=%async_computation.3 | async-start | bytes 8388608
  530.2 27.1 %copy-start.16 = (bf16[2,2,512,512]{2,3,1,0:T(8,128)(2,1)S(1)}, bf16[2,2,512,512]{2,3,1,0:T(8,128)(2,1)}, u32[]{:S(2)}) copy-start(bf16[2,2,512,512]{2,3,1,0:T(8,128)(2,1)} %all-reduce.8.cloned.1.call-done) | copy-start | bytes 6291460
  531.7 30.7 %copy-start.10 = (f32[1,2,2,256,256]{4,3,2,1,0:T(8,128)S(1)}, f32[1,2,2,256,256]{4,3,2,1,0:T(8,128)}, u32[]{:S(2)}) copy-start(f32[1,2,2,256,256]{4,3,2,1,0:T(8,128)} %param.11) | copy-start | bytes 3145732
  531.7 25.6 %collective-permute-start.2 = (bf16[2,2,256,512]{2,3,1,0:T(8,128)(2,1)S(1)}, bf16[2,2,256,512]{2,3,1,0:T(8,128)(2,1)S(1)}, u32[]{:S(2)}, u32[]{:S(2)}) collective-permute-start(bf16[2,2,256,512]{2,3,1,0:T(8,128)(2,1)S(1)} %slice.116), channel_id=1, source_target_pairs={{0,32},{4,36},{8,40},{12,44},{16,48},{20,52},{24,56},{28,60},{32,6... | collective-permute-start | bytes 3145736 | tf_op jit(solution)/shard_map/ppermute | solution.py:16
  557.5 6.8 copy-start.22
  558.4 15.2 %collective-permute-start.3 = (bf16[2,2,256,256]{2,3,1,0:T(8,128)(2,1)}, bf16[2,2,256,256]{2,3,1,0:T(8,128)(2,1)}, u32[]{:S(2)}, u32[]{:S(2)}) collective-permute-start(bf16[2,2,256,256]{2,3,1,0:T(8,128)(2,1)} %slice.159), channel_id=1, source_target_pairs={{0,4},{4,8},{8,12},{12,16},{16,20},{20,24},{24,28},{28,32},{32,36}... | collective-permute-start | bytes 1572872 | tf_op jit(solution)/shard_map/ppermute | solution.py:16
  562.4 7.2 copy-start.24
  563.7 667.4 %copy-start.19 = (f32[4,2,2,4,256]{4,3,2,1,0:T(4,128)S(1)}, f32[4,2,2,4,256]{4,3,2,1,0:T(4,128)}, u32[]{:S(2)}) copy-start(f32[4,2,2,4,256]{4,3,2,1,0:T(4,128)} %param.13) | copy-start | bytes 196612
  563.7 667.4 %copy-start.20 = (f32[4,2,2,4,256]{4,3,2,1,0:T(4,128)S(1)}, f32[4,2,2,4,256]{4,3,2,1,0:T(4,128)}, u32[]{:S(2)}) copy-start(f32[4,2,2,4,256]{4,3,2,1,0:T(4,128)} %param.14) | copy-start | bytes 196612
  566.9 667.1 %copy-start.14 = (f32[1,2,2,256,256]{3,4,2,1,0:T(8,128)S(1)}, f32[1,2,2,256,256]{3,4,2,1,0:T(8,128)}, u32[]{:S(2)}) copy-start(f32[1,2,2,256,256]{3,4,2,1,0:T(8,128)} %copy.196) | copy-start | bytes 3145732
  1237.0 2.6 copy-start.15
  (9 other events, 15.8 us)
Sparse Core Ops, SparseCore 0:
  10.3 256.2 all-gather.1
  306.4 92.8 all-reduce.5
  466.7 63.5 all-reduce.7
  532.7 575.3 all-reduce.9
where the time goes:
time: 1250 us
  waiting for transfers between devices  930 us (74%)
  blocking collectives  121 us (10%)
  matrix products  73.2 us (6%)
  local copies, waits for them, and re-layouts  62.1 us (5%)
  between operations  28.2 us (2%)
  other arithmetic  23.5 us (2%)
    unnamed x5, waiting for transfers between devices  532 us
    all_gather x1, waiting for transfers between devices, body(): lax.all_gather(probe.astype(jnp.bfloat16), 'tile', axis=3, tiled=True)  200 us
    psum x1, blocking collectives, body(): lax.psum((object_sum, probe_sum), ('tile', 'mode'))  121 us
    psum x1, waiting for transfers between devices, body(): power = lax.psum(partial_power, 'mode')  82.1 us
    ppermute x4, waiting for transfers between devices, from_behind(): return lax.ppermute(block, axis, route)  64.6 us
    psum x1, waiting for transfers between devices, body(): lax.psum(region_grad.astype(jnp.bfloat16), 'mode').astype(jnp.float32)  50.8 us
    dot_general x24, matrix products, left_product(): jnp.einsum('ij,...jl->...il', table, right_data, preferred_element_type=j...  35.8 us
    dot_general x24, matrix products, right_product(): jnp.einsum('...jk,kl->...jl', left_data, table, preferred_element_type=jn...  30.7 us
  transfers between devices with their start and end apart: 8, of which 8 were waited for; matrix products, arithmetic and copies ran while one was open for 3% of the time, Pallas kernels for 0%

commit v1 on v0

--- a/solution.py
+++ b/solution.py
@@ -169,7 +169,7 @@
     probe_grad = lax.psum_scatter(probe_local, "tile", scatter_dimension=3, tiled=True)
     object_sum = jnp.sum(tile_grad * tile_grad) / float(mode_count)
     probe_sum = jnp.sum(probe_grad * probe_grad)
-    object_total, probe_total = lax.psum((object_sum, probe_sum), ("tile", "mode"))
+    object_total, probe_total = lax.psum(lax.psum((object_sum, probe_sum), "tile"), "mode")
     object_square = object_total / float(tile_count * layers * 2 * tile_side * tile_side)
     probe_square = probe_total / float(SCAN_COUNT * MODES * 2 * width * width)
     object_direction = -tile_grad[None] + object_square / object_norm_before[0] * object_previous

time: 1250 us -> 1340 us (1.072)
  blocking collectives: 121 us -> 212 us
    psum x1 -> x2, blocking collectives: 121 us -> 212 us  [the longest x1 131 us: body(): lax.psum((object_sum, probe_sum), 'tile')]
where the time goes in v1:
time: 1340 us
  waiting for transfers between devices  929 us (69%)
  blocking collectives  212 us (16%)
  matrix products  73.2 us (5%)
  local copies, waits for them, and re-layouts  62.4 us (5%)
  between operations  28.2 us (2%)
  other arithmetic  23.6 us (2%)
    unnamed x5, waiting for transfers between devices  532 us
    all_gather x1, waiting for transfers between devices, body(): lax.all_gather(probe.astype(jnp.bfloat16), 'tile', axis=3, tiled=True)  200 us
    psum x1, blocking collectives, body(): lax.psum((object_sum, probe_sum), 'tile')  131 us
    psum x1, waiting for transfers between devices, body(): power = lax.psum(partial_power, 'mode')  81.9 us
    psum x1, blocking collectives, body(): lax.psum(lax.psum((object_sum, probe_sum), 'tile'), 'mode')  81.2 us
    ppermute x4, waiting for transfers between devices, from_behind(): return lax.ppermute(block, axis, route)  64.6 us
    psum x1, waiting for transfers between devices, body(): lax.psum(region_grad.astype(jnp.bfloat16), 'mode').astype(jnp.float32)  50.8 us
    dot_general x24, matrix products, left_product(): jnp.einsum('ij,...jl->...il', table, right_data, preferred_element_type=j...  35.8 us
  transfers between devices with their start and end apart: 8, of which 8 were waited for; matrix products, arithmetic and copies ran while one was open for 3% of the time, Pallas kernels for 0%

profile of v1, /device:TPU:1, one launch (start us, length us, event | category | flops | bytes accessed | tf_op | source)
XLA Modules:
  0.0 1338.3 jit_solution(5678504297354861399)
XLA Ops:
  12.1 11.3 collective-permute-done
  27.0 28.2 %collective-permute-done.1 = bf16[2,2,256,512]{3,2,1,0:T(8,128)(2,1)} collective-permute-done((bf16[2,2,256,512]{3,2,1,0:T(8,128)(2,1)S(1)}, bf16[2,2,256,512]{3,2,1,0:T(8,128)(2,1)}, u32[]{:S(2)}, u32[]{:S(2)}) %collective-permute-start.1) | collective-permute-done | bytes 1048608 | tf_op jit(solution)/shard_map/ppermute | solution.py:16
  56.6 6.3 while.1
  66.7 200.1 %all-gather.2.cloned.1.call-done = bf16[4,2,2,256,256]{4,0,2,1,3:T(4,128)(2,1)} async-done(((bf16[4,2,2,4,256]{4,0,2,1,3:T(4,128)(2,1)}), bf16[4,2,2,256,256]{4,0,2,1,3:T(4,128)(2,1)}) %all-gather.2.cloned.1.call-update) | async-done | bytes 2097168 | tf_op jit(solution)/shard_map/all_gather | solution.py:100
  317.3 81.9 %all-reduce.7.cloned.1.call-done = f32[2,256,256]{1,2,0:T(8,128)} async-done(((f32[2,256,256]{1,2,0:T(8,128)}), f32[2,256,256]{1,2,0:T(8,128)}) %all-reduce.7.cloned.1.call-update) | async-done | bytes 524304 | tf_op jit(solution)/shard_map/psum | solution.py:124
  409.8 2.5 add_reduce_fusion
  431.6 3.0 add_bitcast_fusion
  434.9 2.5 broadcast_in_dim.11
  437.4 11.2 dynamic_update_slice.6
  450.4 12.3 dynamic_update_slice.7
  462.7 3.8 convert_element_type.598
  469.6 3.1 copy.197
  472.7 6.6 fusion.156
  479.4 50.8 %all-reduce.9.cloned.1.call-done = bf16[2,2,512,512]{2,3,1,0:T(8,128)(2,1)} async-done(((bf16[2,2,512,512]{2,3,1,0:T(8,128)(2,1)}), bf16[2,2,512,512]{2,3,1,0:T(8,128)(2,1)}) %all-reduce.9.cloned.1.call-update) | async-done | bytes 2097168 | tf_op jit(solution)/shard_map/psum | solution.py:154
  531.7 3.4 collective-permute-start.2
  535.0 22.3 %collective-permute-done.2 = bf16[2,2,256,512]{2,3,1,0:T(8,128)(2,1)S(1)} collective-permute-done((bf16[2,2,256,512]{2,3,1,0:T(8,128)(2,1)S(1)}, bf16[2,2,256,512]{2,3,1,0:T(8,128)(2,1)S(1)}, u32[]{:S(2)}, u32[]{:S(2)}) %collective-permute-start.2) | collective-permute-done | bytes 1048608 | tf_op jit(solution)/shard_map/ppermute | solution.py:16
  558.4 4.0 collective-permute-start.3
  566.9 2.6 copy.195
  570.8 2.8 collective-permute-done.3
  576.2 531.6 %all-reduce.11.cloned.1.call-done = f32[4,2,2,256,256]{4,0,3,2,1:T(4,128)} async-done(((f32[4,2,2,256,256]{4,0,3,2,1:T(4,128)}), f32[4,2,2,256,256]{4,0,3,2,1:T(4,128)}) %all-reduce.11.cloned.1.call-update) | async-done | bytes 4194320
  1109.3 130.5 %all-reduce.1 = (f32[]{:T(128)}, f32[]{:T(128)}) all-reduce(f32[]{:T(128)S(6)} %div.27, f32[]{:T(128)} %multiply_reduce_fusion.1), channel_id=1, replica_groups=mesh['tile'=64,'mode'=4] {'tile'}, use_global_device_ids=true, to_apply=%region_8.9 | all-reduce | flops 2 | bytes 16 | tf_op jit(solution)/shard_map/psum | solution.py:172
  1239.8 81.2 %all-reduce.2 = (f32[]{:T(128)}, f32[]{:T(128)}) all-reduce(f32[]{:T(128)} %get-tuple-element.36, f32[]{:T(128)} %get-tuple-element.37), channel_id=1, replica_groups=mesh['tile'=64,'mode'=4] {'mode'}, use_global_device_ids=true, to_apply=%region_9.10 | all-reduce | flops 2 | bytes 16 | tf_op jit(solution)/shard_map/psum | solution.py:172
  1324.6 2.9 multiply_add_fusion
  1327.5 2.6 copy.200
  (158 shorter events, 108.7 us)
Async XLA Ops:
  7.2 17.8 %copy-start.23 = (s32[2]{0:T(128)S(1)}, s32[2]{0:T(128)}, u32[]{:S(2)}) copy-start(s32[2]{0:T(128)} %param.17) | copy-start | bytes 28
  7.2 259.6 %all-gather.2.cloned.1.call-start = ((), (), s32[]{:S(2)}) async-start(), calls=%async_computation | async-start | bytes 2129920 | tf_op jit(solution)/shard_map/all_gather | solution.py:100
  8.7 390.5 %all-reduce.7.cloned.1.call-start = ((), (), s32[]{:S(2)}) async-start(), calls=%async_computation.1 | async-start | bytes 1048576 | tf_op jit(solution)/shard_map/psum | solution.py:124
  10.1 13.3 collective-permute-start
  23.5 31.7 %collective-permute-start.1 = (bf16[2,2,256,512]{3,2,1,0:T(8,128)(2,1)S(1)}, bf16[2,2,256,512]{3,2,1,0:T(8,128)(2,1)}, u32[]{:S(2)}, u32[]{:S(2)}) collective-permute-start(bf16[2,2,256,512]{3,2,1,0:T(8,128)(2,1)S(1)} %pad_maximum_fusion.3), channel_id=1, source_target_pairs={{32,0},{36,4},{40,8},{44,12},{48,16},{52,20},{56,24},{60,28},{64,3... | collective-permute-start | bytes 3145736 | tf_op jit(solution)/shard_map/ppermute | solution.py:16
  64.4 208.4 %copy-start.2 = (f32[2,256,256]{1,2,0:T(8,128)}, f32[2,256,256]{1,2,0:T(8,128)S(1)}, u32[]{:S(2)}) copy-start(f32[2,256,256]{1,2,0:T(8,128)S(1)} %copy.142) | copy-start | bytes 1572868
  64.6 208.2 %copy-start.4 = (f32[2,256,256]{1,2,0:T(8,128)}, f32[2,256,256]{1,2,0:T(8,128)S(1)}, u32[]{:S(2)}) copy-start(f32[2,256,256]{1,2,0:T(8,128)S(1)} %copy.143) | copy-start | bytes 1572868
  290.0 2.5 copy-start.6
  290.0 2.5 copy-start.8
  306.4 223.8 %all-reduce.9.cloned.1.call-start = ((), (), s32[]{:S(2)}) async-start(), calls=%async_computation.2 | async-start | bytes 4194304 | tf_op jit(solution)/shard_map/psum | solution.py:154
  429.1 2.6 copy-start.1
  429.1 2.6 copy-start.3
  429.1 2.6 copy-start.5
  466.5 641.2 %all-reduce.11.cloned.1.call-start = ((), (), s32[]{:S(2)}) async-start(), calls=%async_computation.3 | async-start | bytes 8388608
  530.2 27.1 %copy-start.16 = (bf16[2,2,512,512]{2,3,1,0:T(8,128)(2,1)S(1)}, bf16[2,2,512,512]{2,3,1,0:T(8,128)(2,1)}, u32[]{:S(2)}) copy-start(bf16[2,2,512,512]{2,3,1,0:T(8,128)(2,1)} %all-reduce.9.cloned.1.call-done) | copy-start | bytes 6291460
  531.6 30.7 %copy-start.10 = (f32[1,2,2,256,256]{4,3,2,1,0:T(8,128)S(1)}, f32[1,2,2,256,256]{4,3,2,1,0:T(8,128)}, u32[]{:S(2)}) copy-start(f32[1,2,2,256,256]{4,3,2,1,0:T(8,128)} %param.11) | copy-start | bytes 3145732
  531.7 25.6 %collective-permute-start.2 = (bf16[2,2,256,512]{2,3,1,0:T(8,128)(2,1)S(1)}, bf16[2,2,256,512]{2,3,1,0:T(8,128)(2,1)S(1)}, u32[]{:S(2)}, u32[]{:S(2)}) collective-permute-start(bf16[2,2,256,512]{2,3,1,0:T(8,128)(2,1)S(1)} %slice.116), channel_id=1, source_target_pairs={{0,32},{4,36},{8,40},{12,44},{16,48},{20,52},{24,56},{28,60},{32,6... | collective-permute-start | bytes 3145736 | tf_op jit(solution)/shard_map/ppermute | solution.py:16
  557.5 6.8 copy-start.22
  558.4 15.2 %collective-permute-start.3 = (bf16[2,2,256,256]{2,3,1,0:T(8,128)(2,1)}, bf16[2,2,256,256]{2,3,1,0:T(8,128)(2,1)}, u32[]{:S(2)}, u32[]{:S(2)}) collective-permute-start(bf16[2,2,256,256]{2,3,1,0:T(8,128)(2,1)} %slice.159), channel_id=1, source_target_pairs={{0,4},{4,8},{8,12},{12,16},{16,20},{20,24},{24,28},{28,32},{32,36}... | collective-permute-start | bytes 1572872 | tf_op jit(solution)/shard_map/ppermute | solution.py:16
  562.3 7.2 copy-start.24
  563.6 758.1 %copy-start.19 = (f32[4,2,2,4,256]{4,3,2,1,0:T(4,128)S(1)}, f32[4,2,2,4,256]{4,3,2,1,0:T(4,128)}, u32[]{:S(2)}) copy-start(f32[4,2,2,4,256]{4,3,2,1,0:T(4,128)} %param.13) | copy-start | bytes 196612
  563.6 758.1 %copy-start.20 = (f32[4,2,2,4,256]{4,3,2,1,0:T(4,128)S(1)}, f32[4,2,2,4,256]{4,3,2,1,0:T(4,128)}, u32[]{:S(2)}) copy-start(f32[4,2,2,4,256]{4,3,2,1,0:T(4,128)} %param.14) | copy-start | bytes 196612
  566.9 757.7 %copy-start.14 = (f32[1,2,2,256,256]{3,4,2,1,0:T(8,128)S(1)}, f32[1,2,2,256,256]{3,4,2,1,0:T(8,128)}, u32[]{:S(2)}) copy-start(f32[1,2,2,256,256]{3,4,2,1,0:T(8,128)} %copy.196) | copy-start | bytes 3145732
  1327.5 2.6 copy-start.15
  (9 other events, 15.8 us)
Sparse Core Ops, SparseCore 0:
  10.3 256.3 all-gather.1
  306.5 92.7 all-reduce.6
  466.7 63.4 all-reduce.8
  532.7 575.0 all-reduce.10
